TPU v7x, 32 devices: a whole 2x2x4 slice. The times are simulated.
32 devices in a mesh: cube: 2 (over y), row: 4 (over x, core), col: 4 (over z).
Axes of the slice: x: 2, y: 2, z: 4, core: 2. Of those that a mesh axis runs over, the one named last changes fastest.
Arguments:
- child_panel: bfloat16 [2, 6144, 256], P('cube', ('row', 'col')), may hold values from -0.75 to 0.75
- child_inverse: float32 [2, 256, 256], P('cube')
- child_trailing: bfloat16 [2, 6144, 6144], P('cube', ('row', 'col')), may hold values from -6 to 6
- child_pattern: int32 [2, 48], P('cube'), may hold values 0 or 1
- child_map: int32 [2, 48], replicated, may hold values from 0 to 95, as said below
- parent_panel: bfloat16 [2, 6144, 256], P('cube', ('row', 'col')), may hold values from -0.75 to 0.75
- parent_inverse: float32 [1, 256, 256], replicated
- parent_trailing: bfloat16 [2, 6144, 12288], P('cube', ('row', 'col')), may hold values from -6 to 6
- parent_pattern: int32 [1, 96], replicated, may hold values 0 or 1
Outputs:
- parent_update: bfloat16 [2, 6144, 12288], P('cube', ('row', 'col'))
Inputs may be any that keep to these rules, and one draw needn't show every extreme that they name: With p = i // 3, child_map[c, i] is one of the blocks h * 48 + p * 3 + k, h in 0 and 1, k from 0 to 2; a child's blocks land on distinct parent blocks.
All inputs are finite; a program needn't handle non-finite values. No bound on the sum of `child_pattern` on one device may be relied on, other than what follows from the above.
Results may differ from a plain program's by a relative error of at most 0.0042.
Values may be sent and summed in bfloat16 or wider, within the bound.
No kernel may reach another device: no remote copies, remote signals or barrier semaphores. Data moves between devices by JAX's collectives and lax.ppermute only.
A program may use at most 192 MiB of HBM per device.

v0:
```python
import jax
import jax.numpy as jnp
from jax import lax
from jax.sharding import PartitionSpec as P

BLOCK = 128


def from_partner(array, axis, apart):
    return lax.ppermute(array, axis, [(i, i ^ 1 << apart) for i in range(lax.axis_size(axis))])


def row_mask(pattern_row, start, how_many):
    window = lax.dynamic_slice_in_dim(pattern_row, start, how_many)
    return jnp.repeat(window, BLOCK).astype(jnp.bfloat16)[:, None]


def one_hot(mapping, extent):
    return (mapping[:, None] == jnp.arange(extent, dtype=jnp.int32)[None, :]).astype(jnp.bfloat16)


def map_columns(values, table):
    row_count = values.shape[0]
    blocks = values.reshape(row_count, table.shape[0], BLOCK)
    shifted = jnp.einsum("rib,ip->rpb", blocks, table, preferred_element_type=jnp.float32)
    return shifted.reshape(row_count, table.shape[1] * BLOCK)


def map_rows(values, table):
    column_count = values.shape[1]
    blocks = values.reshape(table.shape[0], BLOCK, column_count)
    shifted = jnp.einsum("iaw,ip->paw", blocks, table, preferred_element_type=jnp.float32)
    return shifted.reshape(table.shape[1] * BLOCK, column_count)


def contribution(trailing, own_panel, whole_panel, inverse):
    left_factor = jnp.dot(
        own_panel.astype(jnp.float32), inverse, precision=lax.Precision.HIGHEST
    ).astype(jnp.bfloat16)
    update = lax.dot_general(
        left_factor, whole_panel, (((1,), (1,)), ((), ())), preferred_element_type=jnp.float32
    )
    return trailing.astype(jnp.float32) - update


def local(
    child_panel,
    child_inverse,
    child_trailing,
    child_pattern,
    child_map,
    parent_panel,
    parent_inverse,
    parent_trailing,
    parent_pattern,
):
    position = lax.axis_index(("row", "col"))
    cube_index = lax.axis_index("cube")
    half_bit = cube_index % 2
    parent = cube_index // 2
    parent_blocks = parent_pattern.shape[1]
    half_rows = parent_trailing.shape[1] * lax.axis_size(("row", "col"))
    panel_piece = child_panel[0]
    blocks_here = panel_piece.shape[0] // BLOCK
    own_panel = panel_piece * row_mask(child_pattern[0], position * blocks_here, blocks_here)
    whole_panel = lax.all_gather(own_panel, ("row", "col"), axis=0, tiled=True)
    schur_rows = contribution(child_trailing[0], own_panel, whole_panel, child_inverse[0]).astype(
        jnp.bfloat16
    )
    own_map = lax.dynamic_index_in_dim(child_map, cube_index, 0, keepdims=False)
    own_table = one_hot(own_map, parent_blocks)
    widened = map_columns(schur_rows, own_table).astype(jnp.bfloat16)
    spread = lax.all_to_all(widened, ("row", "col"), split_axis=1, concat_axis=0, tiled=True)
    placed = map_rows(spread, own_table).astype(jnp.bfloat16)
    own_half = lax.dynamic_slice_in_dim(placed, half_bit * half_rows, half_rows, 0)
    theirs = lax.dynamic_slice_in_dim(placed, (1 - half_bit) * half_rows, half_rows, 0)
    arrived = from_partner(theirs, "cube", 0)
    summed = (own_half.astype(jnp.float32) + arrived.astype(jnp.float32)).astype(jnp.bfloat16)
    assembled = lax.all_to_all(summed, ("row", "col"), split_axis=0, concat_axis=1, tiled=True)
    parent_piece = parent_panel[0]
    parent_here = parent_piece.shape[0] // BLOCK
    pattern_row = lax.dynamic_index_in_dim(parent_pattern, parent, 0, keepdims=False)
    own_parent = parent_piece * row_mask(
        pattern_row, half_bit * (half_rows // BLOCK) + position * parent_here, parent_here
    )
    half_panel = lax.all_gather(own_parent, ("row", "col"), axis=0, tiled=True)
    other_panel = from_partner(half_panel, "cube", 0)
    whole_parent = jnp.where(
        half_bit == 0,
        jnp.concatenate([half_panel, other_panel], axis=0),
        jnp.concatenate([other_panel, half_panel], axis=0),
    )
    inverse = lax.dynamic_index_in_dim(parent_inverse, parent, 0, keepdims=False)
    result = contribution(parent_trailing[0], own_parent, whole_parent, inverse) + assembled.astype(
        jnp.float32
    )
    return result.astype(jnp.bfloat16)[None]


def solution(mesh):
    in_specs = (
        P("cube", ("row", "col"), None),
        P("cube", None, None),
        P("cube", ("row", "col"), None),
        P("cube", None),
        P(),
        P("cube", ("row", "col"), None),
        P(),
        P("cube", ("row", "col"), None),
        P(),
    )
    out_specs = P("cube", ("row", "col"), None)
    return jax.shard_map(local, mesh=mesh, in_specs=in_specs, out_specs=out_specs, check_vma=False)
```

profile of v0, /device:TPU:0, one launch (start us, length us, event | category | flops | bytes accessed | tf_op | source)
XLA Modules:
  0.0 852.1 jit_solution(2174740888799487291)
XLA Ops:
  6.5 0.0 copy-start
  6.5 0.0 all-gather.5.cloned.1.call-start
  6.5 0.8 fusion.29
  7.3 0.1 broadcast_bitcast_fusion
  7.4 1.7 bitcast_multiply_fusion
  9.1 0.0 all-gather.5.cloned.1.call-update
  9.1 0.7 fusion.27
  9.8 0.0 copy-done
  9.8 1.3 convolution_convert_fusion.1
  11.1 46.5 %all-gather.5.cloned.1.call-done = bf16[6144,256]{1,0:T(8,128)(2,1)} async-done(((bf16[384,256]{1,0:T(8,128)(2,1)}), bf16[6144,256]{1,0:T(8,128)(2,1)}) %all-gather.5.cloned.1.call-update) | async-done | bytes 3145744 | tf_op jit(solution)/shard_map/all_gather | solution.py:66
  57.6 4.7 fusion.11
  62.3 1.3 copy.15
  63.6 5.2 convert_bitcast_fusion.1
  68.8 16.8 %convert_element_type.104 = bf16[384,16,768]{2,1,0:T(8,128)(2,1)} reshape(bf16[384,96,128]{2,1,0:T(8,128)(2,1)} %convert_bitcast_fusion.1) | data formatting | bytes 18874368 | tf_op jit(solution)/shard_map/convert_element_type | solution.py:72
  85.6 10.7 %copy.10 = bf16[384,16,768]{2,0,1:T(8,128)(2,1)} copy(bf16[384,16,768]{2,1,0:T(8,128)(2,1)} %convert_element_type.104) | data formatting | bytes 18874368 | tf_op jit(solution)/shard_map/convert_element_type | solution.py:72
  96.3 5.0 all-to-all-start
  101.3 206.5 %all-to-all-done = bf16[384,16,768]{2,0,1:T(8,128)(2,1)} async-done(((bf16[384,16,768]{2,0,1:T(8,128)(2,1)}), bf16[384,16,768]{2,0,1:T(8,128)(2,1)}, u32[]{:S(2)}, u32[]{:S(2)}) %all-to-all-start) | async-done | bytes 9437216 | tf_op jit(solution)/shard_map/all_to_all | solution.py:73
  307.9 16.0 %convolution_convert_fusion = bf16[96,128,768]{2,0,1:T(8,128)(2,1)} fusion(bf16[48,128,768]{2,1,0:T(8,128)(2,1)} %bitcast.16, s32[48]{0:T(128)S(1)} %fusion.27), kind=kOutput, calls=%fused_computation.6 | convolution fusion | flops 915411456 | bytes 28311744 | tf_op jit(solution)/shard_map/iaw,ip->paw/dot_general | solution.py:32
  323.9 20.2 %copy.12 = bf16[96,128,768]{2,1,0:T(8,128)(2,1)} copy(bf16[96,128,768]{2,0,1:T(8,128)(2,1)} %convolution_convert_fusion) | data formatting | bytes 37748736 | tf_op jit(solution)/shard_map/convert_element_type | solution.py:74
  344.1 8.0 constant_dynamic-slice_fusion
  352.1 1.5 collective-permute-start.1
  353.7 203.2 %collective-permute-done.1 = bf16[6144,768]{1,0:T(8,128)(2,1)} collective-permute-done((bf16[6144,768]{1,0:T(8,128)(2,1)}, bf16[6144,768]{1,0:T(8,128)(2,1)}, u32[]{:S(2)}, u32[]{:S(2)}) %collective-permute-start.1) | collective-permute-done | bytes 9437216 | tf_op jit(solution)/shard_map/ppermute | solution.py:10
  556.9 11.9 %add_convert_fusion = bf16[6144,768]{1,0:T(8,128)(2,1)} fusion(bf16[6144,768]{1,0:T(8,128)(2,1)} %collective-permute-done.1, bf16[12288,768]{1,0:T(8,128)(2,1)} %bitcast.60, s32[]{:T(128)S(6)} %select_n.43), kind=kLoop, calls=%fused_computation.4 | loop fusion | flops 18874368 | bytes 28311556 | tf_op jit(solution)/shard_map/convert_element_type | solution.py:78
  568.8 0.0 copy-start.5
  568.8 0.0 copy-start.3
  568.8 0.0 copy-start.4
  568.8 4.9 all-to-all-start.1
  573.8 0.3 all-gather.3.cloned.1.call-start
  574.1 0.0 copy-done.5
  574.1 0.1 fusion.26
  574.1 0.1 broadcast_bitcast_fusion.1
  574.2 0.0 copy-done.3
  574.2 0.8 bitcast_multiply_fusion.1
  575.0 0.0 all-gather.3.cloned.1.call-update
  575.1 157.3 %all-gather.3.cloned.1.call-done = bf16[6144,256]{1,0:T(8,128)(2,1)} async-done(((bf16[384,256]{1,0:T(8,128)(2,1)}), bf16[6144,256]{1,0:T(8,128)(2,1)}) %all-gather.3.cloned.1.call-update) | async-done | bytes 3145744 | tf_op jit(solution)/shard_map/all_gather | solution.py:86
  732.4 1.5 collective-permute-start
  733.9 0.0 copy-done.4
  733.9 1.0 convolution_convert_fusion.2
  734.9 64.5 %all-to-all-done.1 = bf16[16,384,768]{2,1,0:T(8,128)(2,1)} async-done(((bf16[16,384,768]{2,1,0:T(8,128)(2,1)}), bf16[16,384,768]{2,1,0:T(8,128)(2,1)}, u32[]{:S(2)}, u32[]{:S(2)}) %all-to-all-start.1) | async-done | bytes 9437216 | tf_op jit(solution)/shard_map/all_to_all | solution.py:79
  799.5 12.2 %convert_bitcast_fusion = f32[16,48,8,768]{3,2,1,0:T(8,128)} fusion(bf16[16,384,768]{2,1,0:T(8,128)(2,1)} %all-to-all-done.1), kind=kLoop, calls=%fused_computation.3 | loop fusion | flops 4718592 | bytes 28311552
  811.7 0.0 copy-start.2
  811.7 12.9 %copy.14 = f32[16,48,8,768]{3,2,0,1:T(8,128)} copy(f32[16,48,8,768]{3,2,1,0:T(8,128)} %convert_bitcast_fusion) | data formatting | bytes 37748736 | tf_op jit(solution)/shard_map/convert_element_type | solution.py:94
  824.6 0.0 collective-permute-done
  824.6 0.0 copy-done.2
  824.6 0.0 copy-start.1
  824.6 20.6 %fusion.2 = bf16[1,384,12288]{2,1,0:T(8,128)(2,1)} fusion(f32[384,12288]{1,0:T(8,128)} %bitcast.58, bf16[384,256]{1,0:T(8,128)(2,1)} %convolution_convert_fusion.2, bf16[1,384,12288]{2,1,0:T(8,128)(2,1)} %param.16, bf16[6144,256]{1,0:T(8,128)(2,1)} %collective-permute-done, bf16[6144,256]{1,0:T(8,128)(2,1)S(1)} %copy-done.2, pred[]{:T(512)S(6)} %eq.20), kind=kOutput, calls=%fused_computation.5 | convolution fusion | flops 2463105024 | bytes 44236800 | tf_op jit(solution)/shard_map/dot_general | solution.py:40
  845.2 0.0 copy-done.1
Async XLA Ops:
  6.5 3.3 copy-start
  6.5 51.0 %all-gather.5.cloned.1.call-start = ((), (), s32[]{:S(2)}) async-start(), calls=%async_computation.3 | async-start | bytes 3342336 | tf_op jit(solution)/shard_map/all_gather | solution.py:66
  96.3 211.5 %all-to-all-start = ((bf16[384,16,768]{2,0,1:T(8,128)(2,1)}), bf16[384,16,768]{2,0,1:T(8,128)(2,1)}, u32[]{:S(2)}, u32[]{:S(2)}) async-start(bf16[384,16,768]{2,0,1:T(8,128)(2,1)} %copy.10), calls=%async_computation | async-start | bytes 18874368 | tf_op jit(solution)/shard_map/all_to_all | solution.py:73
  352.1 204.8 %collective-permute-start.1 = (bf16[6144,768]{1,0:T(8,128)(2,1)}, bf16[6144,768]{1,0:T(8,128)(2,1)}, u32[]{:S(2)}, u32[]{:S(2)}) collective-permute-start(bf16[6144,768]{1,0:T(8,128)(2,1)} %constant_dynamic-slice_fusion), channel_id=1, source_target_pairs={{0,16},{16,0},{1,17},{17,1},{2,18},{18,2},{3,19},{19,3},{4,20},{20... | collective-permute-start | bytes 28311560 | tf_op jit(solution)/shard_map/ppermute | solution.py:10
  568.8 5.2 copy-start.5
  568.8 5.4 copy-start.3
  568.8 165.1 %copy-start.4 = (f32[1,256,256]{2,1,0:T(8,128)S(1)}, f32[1,256,256]{2,1,0:T(8,128)}, u32[]{:S(2)}) copy-start(f32[1,256,256]{2,1,0:T(8,128)} %param.15) | copy-start | bytes 786436
  568.8 230.6 %all-to-all-start.1 = ((bf16[16,384,768]{2,1,0:T(8,128)(2,1)}), bf16[16,384,768]{2,1,0:T(8,128)(2,1)}, u32[]{:S(2)}, u32[]{:S(2)}) async-start(bf16[16,384,768]{2,1,0:T(8,128)(2,1)} %bitcast.61), calls=%async_computation.1 | async-start | bytes 18874368 | tf_op jit(solution)/shard_map/all_to_all | solution.py:79
  573.8 158.6 %all-gather.3.cloned.1.call-start = ((), (), s32[]{:S(2)}) async-start(), calls=%async_computation.2 | async-start | bytes 3342336 | tf_op jit(solution)/shard_map/all_gather | solution.py:86
  732.4 92.2 %collective-permute-start = (bf16[6144,256]{1,0:T(8,128)(2,1)}, bf16[6144,256]{1,0:T(8,128)(2,1)}, u32[]{:S(2)}, u32[]{:S(2)}) collective-permute-start(bf16[6144,256]{1,0:T(8,128)(2,1)} %all-gather.3.cloned.1.call-done), channel_id=1, source_target_pairs={{0,16},{16,0},{1,17},{17,1},{2,18},{18,2},{3,19},{19,3},{4,20},{20... | collective-permute-start | bytes 9437192 | tf_op jit(solution)/shard_map/ppermute | solution.py:10
  811.7 12.9 %copy-start.2 = (bf16[6144,256]{1,0:T(8,128)(2,1)S(1)}, bf16[6144,256]{1,0:T(8,128)(2,1)}, u32[]{:S(2)}) copy-start(bf16[6144,256]{1,0:T(8,128)(2,1)} %all-gather.3.cloned.1.call-done) | copy-start | bytes 9437188
  824.6 20.6 %copy-start.1 = (f32[1,256,256]{2,1,0:T(8,128)S(1)}, f32[1,256,256]{2,1,0:T(8,128)}, u32[]{:S(2)}) copy-start(f32[1,256,256]{2,1,0:T(8,128)} %param.10) | copy-start | bytes 786436
Sparse Core Ops, SparseCore 0:
  9.7 47.8 all-gather.4
  576.9 155.3 all-gather.2
where the time goes:
time: 853 us; the launch traced here: 852 us
  waiting for transfers between devices  678 us (79%)
  local copies, waits for them, and re-layouts  70.8 us (8%)
  matrix products  48.9 us (6%)
  other arithmetic  27.5 us (3%)
  between operations  13.5 us (2%)
  starting transfers between devices  13.2 us (2%)
    all_to_all x1, waiting for transfers between devices, local(): lax.all_to_all(widened, ('row', 'col'), split_axis=1, concat_axis=0, tile...  207 us
    ppermute x2, waiting for transfers between devices, from_partner(): lax.ppermute(array, axis, [(i, i ^ 1 << apart) for i in range(lax.axis_si...  203 us
    all_gather x1, waiting for transfers between devices, local(): half_panel = lax.all_gather(own_parent, ('row', 'col'), axis=0, tiled=True)  157 us
    all_to_all x1, waiting for transfers between devices, local(): lax.all_to_all(summed, ('row', 'col'), split_axis=0, concat_axis=1, tiled...  64.5 us
    all_gather x1, waiting for transfers between devices, local(): whole_panel = lax.all_gather(own_panel, ('row', 'col'), axis=0, tiled=True)  46.5 us
    convert_element_type x2, local copies, waits for them, and re-layouts, local(): widened = map_columns(schur_rows, own_table).astype(jnp.bfloat16)  27.5 us
    dot_general x2, matrix products, contribution(): lax.dot_general(left_factor, whole_panel, (((1,), (1,)), ((), ())), prefe...  25.3 us
    convert_element_type x1, local copies, waits for them, and re-layouts, local(): placed = map_rows(spread, own_table).astype(jnp.bfloat16)  20.2 us
  transfers between devices with their start and end apart: 6, of which 5 were waited for; matrix products, arithmetic and copies ran while one was open for 3% of the time, Pallas kernels for 0%

commit v1 on v0

--- a/solution.py
+++ b/solution.py
@@ -63,7 +63,29 @@
     panel_piece = child_panel[0]
     blocks_here = panel_piece.shape[0] // BLOCK
     own_panel = panel_piece * row_mask(child_pattern[0], position * blocks_here, blocks_here)
-    whole_panel = lax.all_gather(own_panel, ("row", "col"), axis=0, tiled=True)
+    ways, here, hop = (
+        lax.axis_size(("row", "col")),
+        lax.axis_index(("row", "col")),
+        own_panel.shape[0],
+    )
+    dims = [n * ways if d == 0 else n for d, n in enumerate(own_panel.shape)]
+    full = lax.dynamic_update_slice_in_dim(
+        jnp.zeros(dims, own_panel.dtype), own_panel, here * hop, axis=0
+    )
+    going_up = going_down = own_panel
+    for far in range(1, ways // 2 + 1):
+        going_up = lax.ppermute(
+            going_up, ("row", "col"), [(d, (d + 1) % ways) for d in range(ways)]
+        )
+        full = lax.dynamic_update_slice_in_dim(full, going_up, (here - far) % ways * hop, axis=0)
+        if 2 * far < ways:
+            going_down = lax.ppermute(
+                going_down, ("row", "col"), [(d, (d - 1) % ways) for d in range(ways)]
+            )
+            full = lax.dynamic_update_slice_in_dim(
+                full, going_down, (here + far) % ways * hop, axis=0
+            )
+    whole_panel = full
     schur_rows = contribution(child_trailing[0], own_panel, whole_panel, child_inverse[0]).astype(
         jnp.bfloat16
     )

time: 853 us -> 885 us (1.038)
  starting transfers between devices: 13.2 us -> 70.3 us
  waiting for transfers between devices: 678 us -> 653 us
    ppermute x0 -> x15, starting transfers between devices: none -> 55.7 us  [the longest x8 47.3 us: local(): lax.ppermute(going_up, ('row', 'col'), [(d, (d + 1) % ways) for d in rang...]
    all_gather x1 -> x0, waiting for transfers between devices: 46.5 us -> none  [local(): whole_panel = lax.all_gather(own_panel, ('row', 'col'), axis=0, tiled=True)]
    ppermute x0 -> x15, waiting for transfers between devices: none -> 21.4 us  [the longest x8 17.1 us: local(): lax.ppermute(going_up, ('row', 'col'), [(d, (d + 1) % ways) for d in rang...]
  transfers between devices with their start and end apart: 6 -> 20, of which waited for: 5 -> 14; matrix products, arithmetic and copies ran while one was open for 3% -> 4% of each run, Pallas kernels for 0% -> 0%
where the time goes in v1:
time: 885 us; the launch traced here: 884 us
  waiting for transfers between devices  653 us (74%)
  local copies, waits for them, and re-layouts  73.2 us (8%)
  starting transfers between devices  70.3 us (8%)
  matrix products  45.5 us (5%)
  other arithmetic  27.5 us (3%)
  between operations  13.6 us (2%)
    all_to_all x1, waiting for transfers between devices, local(): lax.all_to_all(widened, ('row', 'col'), split_axis=1, concat_axis=0, tile...  207 us
    ppermute x2, waiting for transfers between devices, from_partner(): lax.ppermute(array, axis, [(i, i ^ 1 << apart) for i in range(lax.axis_si...  203 us
    all_gather x1, waiting for transfers between devices, local(): half_panel = lax.all_gather(own_parent, ('row', 'col'), axis=0, tiled=True)  157 us
    all_to_all x1, waiting for transfers between devices, local(): lax.all_to_all(summed, ('row', 'col'), split_axis=0, concat_axis=1, tiled...  64.6 us
    ppermute x8, starting transfers between devices, local(): lax.ppermute(going_up, ('row', 'col'), [(d, (d + 1) % ways) for d in rang...  47.3 us
    convert_element_type x2, local copies, waits for them, and re-layouts, local(): widened = map_columns(schur_rows, own_table).astype(jnp.bfloat16)  27.5 us
    dot_general x2, matrix products, contribution(): lax.dot_general(left_factor, whole_panel, (((1,), (1,)), ((), ())), prefe...  22 us
    convert_element_type x1, local copies, waits for them, and re-layouts, local(): placed = map_rows(spread, own_table).astype(jnp.bfloat16)  20.1 us
  transfers between devices with their start and end apart: 20, of which 14 were waited for; matrix products, arithmetic and copies ran while one was open for 4% of the time, Pallas kernels for 0%

profile of v1, /device:TPU:0, one launch (start us, length us, event | category | flops | bytes accessed | tf_op | source)
XLA Modules:
  0.0 883.6 jit_solution(324860102933984802)
XLA Ops:
  6.5 0.8 fusion.29
  7.3 0.1 broadcast_bitcast_fusion
  7.4 0.2 broadcast_in_dim.18
  7.6 1.7 constant_dynamic-update-slice_fusion.15
  9.3 3.0 collective-permute-start.1
  12.3 2.4 collective-permute-start.2
  14.7 0.8 fusion.27
  15.6 1.5 convolution_convert_fusion.1
  17.1 2.8 collective-permute-done.1
  19.8 0.6 collective-permute-start.3
  20.5 2.8 collective-permute-done.2
  23.2 2.9 collective-permute-start.4
  26.1 0.9 constant_dynamic-update-slice_fusion.14
  27.0 0.9 constant_dynamic-update-slice_fusion.13
  28.0 0.0 collective-permute-done.3
  28.0 4.9 collective-permute-start.5
  32.9 0.9 collective-permute-done.4
  33.9 1.2 collective-permute-start.6
  35.1 1.2 collective-permute-done.5
  36.3 7.6 collective-permute-start.7
  43.9 0.6 collective-permute-done.6
  44.6 0.1 collective-permute-start.8
  44.7 2.4 collective-permute-done.7
  47.1 8.6 collective-permute-start.9
  55.7 0.0 collective-permute-done.8
  55.7 0.0 collective-permute-start.10
  55.8 3.1 collective-permute-done.9
  58.9 7.9 collective-permute-start.11
  66.8 0.0 collective-permute-done.10
  66.8 0.4 collective-permute-start.12
  67.3 2.7 collective-permute-done.11
  70.0 7.1 collective-permute-start.13
  77.1 1.4 collective-permute-start.14
  78.6 1.7 collective-permute-done.13
  80.3 7.5 collective-permute-start.15
  87.8 0.0 collective-permute-done.14
  87.9 3.1 collective-permute-done.15
  91.0 1.5 fusion.11
  92.5 1.3 copy.15
  93.8 5.2 convert_bitcast_fusion.1
  99.0 16.8 %convert_element_type.104 = bf16[384,16,768]{2,1,0:T(8,128)(2,1)} reshape(bf16[384,96,128]{2,1,0:T(8,128)(2,1)} %convert_bitcast_fusion.1) | data formatting | bytes 18874368 | tf_op jit(solution)/shard_map/convert_element_type | solution.py:94
  115.9 10.7 %copy.10 = bf16[384,16,768]{2,0,1:T(8,128)(2,1)} copy(bf16[384,16,768]{2,1,0:T(8,128)(2,1)} %convert_element_type.104) | data formatting | bytes 18874368 | tf_op jit(solution)/shard_map/convert_element_type | solution.py:94
  126.6 6.4 all-to-all-start
  133.0 206.8 %all-to-all-done = bf16[384,16,768]{2,0,1:T(8,128)(2,1)} async-done(((bf16[384,16,768]{2,0,1:T(8,128)(2,1)}), bf16[384,16,768]{2,0,1:T(8,128)(2,1)}, u32[]{:S(2)}, u32[]{:S(2)}) %all-to-all-start) | async-done | bytes 9437216 | tf_op jit(solution)/shard_map/all_to_all | solution.py:95
  339.7 15.8 %convolution_convert_fusion = bf16[96,128,768]{2,0,1:T(8,128)(2,1)} fusion(bf16[48,128,768]{2,1,0:T(8,128)(2,1)} %bitcast.16, s32[48]{0:T(128)S(1)} %fusion.27), kind=kOutput, calls=%fused_computation.6 | convolution fusion | flops 915411456 | bytes 28311744 | tf_op jit(solution)/shard_map/iaw,ip->paw/dot_general | solution.py:32
  355.6 20.1 %copy.12 = bf16[96,128,768]{2,1,0:T(8,128)(2,1)} copy(bf16[96,128,768]{2,0,1:T(8,128)(2,1)} %convolution_convert_fusion) | data formatting | bytes 37748736 | tf_op jit(solution)/shard_map/convert_element_type | solution.py:96
  375.7 8.0 constant_dynamic-slice_fusion
  383.7 1.5 collective-permute-start.16
  385.2 203.3 %collective-permute-done.16 = bf16[6144,768]{1,0:T(8,128)(2,1)} collective-permute-done((bf16[6144,768]{1,0:T(8,128)(2,1)}, bf16[6144,768]{1,0:T(8,128)(2,1)}, u32[]{:S(2)}, u32[]{:S(2)}) %collective-permute-start.16) | collective-permute-done | bytes 9437216 | tf_op jit(solution)/shard_map/ppermute | solution.py:10
  588.5 11.9 %add_convert_fusion = bf16[6144,768]{1,0:T(8,128)(2,1)} fusion(bf16[6144,768]{1,0:T(8,128)(2,1)} %collective-permute-done.16, bf16[12288,768]{1,0:T(8,128)(2,1)} %bitcast.61, s32[]{:T(128)S(6)} %select_n.182), kind=kLoop, calls=%fused_computation.4 | loop fusion | flops 18874368 | bytes 28311556 | tf_op jit(solution)/shard_map/convert_element_type | solution.py:100
  600.5 4.9 all-to-all-start.1
  605.4 0.3 all-gather.2.cloned.1.call-start
  605.7 0.1 fusion.26
  605.8 0.1 broadcast_bitcast_fusion.1
  605.9 0.8 bitcast_multiply_fusion.1
  606.7 0.0 all-gather.2.cloned.1.call-update
  606.7 157.3 %all-gather.2.cloned.1.call-done = bf16[6144,256]{1,0:T(8,128)(2,1)} async-done(((bf16[384,256]{1,0:T(8,128)(2,1)}), bf16[6144,256]{1,0:T(8,128)(2,1)}) %all-gather.2.cloned.1.call-update) | async-done | bytes 3145744 | tf_op jit(solution)/shard_map/all_gather | solution.py:108
  764.0 1.5 collective-permute-start
  765.5 1.0 convolution_convert_fusion.2
  766.5 64.6 %all-to-all-done.1 = bf16[16,384,768]{2,1,0:T(8,128)(2,1)} async-done(((bf16[16,384,768]{2,1,0:T(8,128)(2,1)}), bf16[16,384,768]{2,1,0:T(8,128)(2,1)}, u32[]{:S(2)}, u32[]{:S(2)}) %all-to-all-start.1) | async-done | bytes 9437216 | tf_op jit(solution)/shard_map/all_to_all | solution.py:101
  831.1 12.2 %convert_bitcast_fusion = f32[16,48,8,768]{3,2,1,0:T(8,128)} fusion(bf16[16,384,768]{2,1,0:T(8,128)(2,1)} %all-to-all-done.1), kind=kLoop, calls=%fused_computation.3 | loop fusion | flops 4718592 | bytes 28311552
  843.3 12.9 %copy.14 = f32[16,48,8,768]{3,2,0,1:T(8,128)} copy(f32[16,48,8,768]{3,2,1,0:T(8,128)} %convert_bitcast_fusion) | data formatting | bytes 37748736 | tf_op jit(solution)/shard_map/convert_element_type | solution.py:116
  856.2 0.0 collective-permute-done
  856.2 20.5 %fusion.2 = bf16[1,384,12288]{2,1,0:T(8,128)(2,1)} fusion(f32[384,12288]{1,0:T(8,128)} %bitcast.59, bf16[384,256]{1,0:T(8,128)(2,1)} %convolution_convert_fusion.2, bf16[1,384,12288]{2,1,0:T(8,128)(2,1)} %param.16, bf16[6144,256]{1,0:T(8,128)(2,1)} %collective-permute-done, bf16[6144,256]{1,0:T(8,128)(2,1)S(1)} %copy-done.3, pred[]{:T(512)S(6)} %eq.35), kind=kOutput, calls=%fused_computation.5 | convolution fusion | flops 2463105024 | bytes 44236800 | tf_op jit(solution)/shard_map/dot_general | solution.py:40
  (28 shorter events, 0.3 us)
Async XLA Ops:
  6.5 9.0 %copy-start = (f32[1,256,256]{2,1,0:T(8,128)S(1)}, f32[1,256,256]{2,1,0:T(8,128)}, u32[]{:S(2)}) copy-start(f32[1,256,256]{2,1,0:T(8,128)} %param.10) | copy-start | bytes 786436
  9.3 10.5 %collective-permute-start.1 = (bf16[384,256]{1,0:T(8,128)(2,1)}, bf16[384,256]{1,0:T(8,128)(2,1)}, u32[]{:S(2)}, u32[]{:S(2)}) collective-permute-start(bf16[384,256]{1,0:T(8,128)(2,1)} %get-tuple-element.6), channel_id=1, source_target_pairs={{0,1},{1,2},{2,3},{3,4},{4,5},{5,6},{6,7},{7,8},{8,9},{9,10},{10,1... | collective-permute-start | bytes 589832 | tf_op jit(solution)/shard_map/ppermute | solution.py:77
  12.3 10.9 %collective-permute-start.2 = (bf16[384,256]{1,0:T(8,128)(2,1)}, bf16[384,256]{1,0:T(8,128)(2,1)}, u32[]{:S(2)}, u32[]{:S(2)}) collective-permute-start(bf16[384,256]{1,0:T(8,128)(2,1)} %get-tuple-element.6), channel_id=1, source_target_pairs={{0,15},{1,0},{2,1},{3,2},{4,3},{5,4},{6,5},{7,6},{8,7},{9,8},{10,9... | collective-permute-start | bytes 589832 | tf_op jit(solution)/shard_map/ppermute | solution.py:82
  14.7 76.3 %copy-start.2 = (bf16[1,384,6144]{2,1,0:T(8,128)(2,1)S(1)}, bf16[1,384,6144]{2,1,0:T(8,128)(2,1)}, u32[]{:S(2)}) copy-start(bf16[1,384,6144]{2,1,0:T(8,128)(2,1)} %param.11) | copy-start | bytes 14155780
  19.8 8.2 collective-permute-start.3
  23.2 10.6 %collective-permute-start.4 = (bf16[384,256]{1,0:T(8,128)(2,1)}, bf16[384,256]{1,0:T(8,128)(2,1)S(1)}, u32[]{:S(2)}, u32[]{:S(2)}) collective-permute-start(bf16[384,256]{1,0:T(8,128)(2,1)} %collective-permute-done.2), channel_id=1, source_target_pairs={{0,15},{1,0},{2,1},{3,2},{4,3},{5,4},{6,5},{7,6},{8,7},{9,8},{10,9... | collective-permute-start | bytes 589832 | tf_op jit(solution)/shard_map/ppermute | solution.py:82
  28.0 8.3 collective-permute-start.5
  33.9 10.7 %collective-permute-start.6 = (bf16[384,256]{1,0:T(8,128)(2,1)S(1)}, bf16[384,256]{1,0:T(8,128)(2,1)S(1)}, u32[]{:S(2)}, u32[]{:S(2)}) collective-permute-start(bf16[384,256]{1,0:T(8,128)(2,1)S(1)} %collective-permute-done.4), channel_id=1, source_target_pairs={{0,15},{1,0},{2,1},{3,2},{4,3},{5,4},{6,5},{7,6},{8,7},{9,8},{10,9... | collective-permute-start | bytes 589832 | tf_op jit(solution)/shard_map/ppermute | solution.py:82
  36.3 10.8 %collective-permute-start.7 = (bf16[384,256]{1,0:T(8,128)(2,1)S(1)}, bf16[384,256]{1,0:T(8,128)(2,1)S(1)}, u32[]{:S(2)}, u32[]{:S(2)}) collective-permute-start(bf16[384,256]{1,0:T(8,128)(2,1)S(1)} %collective-permute-done.5), channel_id=1, source_target_pairs={{0,1},{1,2},{2,3},{3,4},{4,5},{5,6},{6,7},{7,8},{8,9},{9,10},{10,1... | collective-permute-start | bytes 589832 | tf_op jit(solution)/shard_map/ppermute | solution.py:77
  44.6 11.1 %collective-permute-start.8 = (bf16[384,256]{1,0:T(8,128)(2,1)S(1)}, bf16[384,256]{1,0:T(8,128)(2,1)S(1)}, u32[]{:S(2)}, u32[]{:S(2)}) collective-permute-start(bf16[384,256]{1,0:T(8,128)(2,1)S(1)} %collective-permute-done.6), channel_id=1, source_target_pairs={{0,15},{1,0},{2,1},{3,2},{4,3},{5,4},{6,5},{7,6},{8,7},{9,8},{10,9... | collective-permute-start | bytes 589832 | tf_op jit(solution)/shard_map/ppermute | solution.py:82
  47.1 11.7 %collective-permute-start.9 = (bf16[384,256]{1,0:T(8,128)(2,1)S(1)}, bf16[384,256]{1,0:T(8,128)(2,1)S(1)}, u32[]{:S(2)}, u32[]{:S(2)}) collective-permute-start(bf16[384,256]{1,0:T(8,128)(2,1)S(1)} %collective-permute-done.7), channel_id=1, source_target_pairs={{0,1},{1,2},{2,3},{3,4},{4,5},{5,6},{6,7},{7,8},{8,9},{9,10},{10,1... | collective-permute-start | bytes 589832 | tf_op jit(solution)/shard_map/ppermute | solution.py:77
  55.7 11.1 %collective-permute-start.10 = (bf16[384,256]{1,0:T(8,128)(2,1)S(1)}, bf16[384,256]{1,0:T(8,128)(2,1)S(1)}, u32[]{:S(2)}, u32[]{:S(2)}) collective-permute-start(bf16[384,256]{1,0:T(8,128)(2,1)S(1)} %collective-permute-done.8), channel_id=1, source_target_pairs={{0,15},{1,0},{2,1},{3,2},{4,3},{5,4},{6,5},{7,6},{8,7},{9,8},{10,9... | collective-permute-start | bytes 589832 | tf_op jit(solution)/shard_map/ppermute | solution.py:82
  58.9 11.1 %collective-permute-start.11 = (bf16[384,256]{1,0:T(8,128)(2,1)S(1)}, bf16[384,256]{1,0:T(8,128)(2,1)S(1)}, u32[]{:S(2)}, u32[]{:S(2)}) collective-permute-start(bf16[384,256]{1,0:T(8,128)(2,1)S(1)} %collective-permute-done.9), channel_id=1, source_target_pairs={{0,1},{1,2},{2,3},{3,4},{4,5},{5,6},{6,7},{7,8},{8,9},{9,10},{10,1... | collective-permute-start | bytes 589832 | tf_op jit(solution)/shard_map/ppermute | solution.py:77
  66.8 10.3 %collective-permute-start.12 = (bf16[384,256]{1,0:T(8,128)(2,1)S(1)}, bf16[384,256]{1,0:T(8,128)(2,1)S(1)}, u32[]{:S(2)}, u32[]{:S(2)}) collective-permute-start(bf16[384,256]{1,0:T(8,128)(2,1)S(1)} %collective-permute-done.10), channel_id=1, source_target_pairs={{0,15},{1,0},{2,1},{3,2},{4,3},{5,4},{6,5},{7,6},{8,7},{9,8},{10,9... | collective-permute-start | bytes 589832 | tf_op jit(solution)/shard_map/ppermute | solution.py:82
  70.0 10.3 %collective-permute-start.13 = (bf16[384,256]{1,0:T(8,128)(2,1)S(1)}, bf16[384,256]{1,0:T(8,128)(2,1)S(1)}, u32[]{:S(2)}, u32[]{:S(2)}) collective-permute-start(bf16[384,256]{1,0:T(8,128)(2,1)S(1)} %collective-permute-done.11), channel_id=1, source_target_pairs={{0,1},{1,2},{2,3},{3,4},{4,5},{5,6},{6,7},{7,8},{8,9},{9,10},{10,1... | collective-permute-start | bytes 589832 | tf_op jit(solution)/shard_map/ppermute | solution.py:77
  77.1 10.7 %collective-permute-start.14 = (bf16[384,256]{1,0:T(8,128)(2,1)S(1)}, bf16[384,256]{1,0:T(8,128)(2,1)S(1)}, u32[]{:S(2)}, u32[]{:S(2)}) collective-permute-start(bf16[384,256]{1,0:T(8,128)(2,1)S(1)} %collective-permute-done.12), channel_id=1, source_target_pairs={{0,15},{1,0},{2,1},{3,2},{4,3},{5,4},{6,5},{7,6},{8,7},{9,8},{10,9... | collective-permute-start | bytes 589832 | tf_op jit(solution)/shard_map/ppermute | solution.py:82
  80.3 10.7 %collective-permute-start.15 = (bf16[384,256]{1,0:T(8,128)(2,1)S(1)}, bf16[384,256]{1,0:T(8,128)(2,1)S(1)}, u32[]{:S(2)}, u32[]{:S(2)}) collective-permute-start(bf16[384,256]{1,0:T(8,128)(2,1)S(1)} %collective-permute-done.13), channel_id=1, source_target_pairs={{0,1},{1,2},{2,3},{3,4},{4,5},{5,6},{6,7},{7,8},{8,9},{9,10},{10,1... | collective-permute-start | bytes 589832 | tf_op jit(solution)/shard_map/ppermute | solution.py:77
  126.6 213.2 %all-to-all-start = ((bf16[384,16,768]{2,0,1:T(8,128)(2,1)}), bf16[384,16,768]{2,0,1:T(8,128)(2,1)}, u32[]{:S(2)}, u32[]{:S(2)}) async-start(bf16[384,16,768]{2,0,1:T(8,128)(2,1)} %copy.10), calls=%async_computation | async-start | bytes 18874368 | tf_op jit(solution)/shard_map/all_to_all | solution.py:95
  383.7 204.8 %collective-permute-start.16 = (bf16[6144,768]{1,0:T(8,128)(2,1)}, bf16[6144,768]{1,0:T(8,128)(2,1)}, u32[]{:S(2)}, u32[]{:S(2)}) collective-permute-start(bf16[6144,768]{1,0:T(8,128)(2,1)} %constant_dynamic-slice_fusion), channel_id=1, source_target_pairs={{0,16},{16,0},{1,17},{17,1},{2,18},{18,2},{3,19},{19,3},{4,20},{20... | collective-permute-start | bytes 28311560 | tf_op jit(solution)/shard_map/ppermute | solution.py:10
  600.5 5.2 copy-start.6
  600.5 5.4 copy-start.4
  600.5 165.0 %copy-start.5 = (f32[1,256,256]{2,1,0:T(8,128)S(1)}, f32[1,256,256]{2,1,0:T(8,128)}, u32[]{:S(2)}) copy-start(f32[1,256,256]{2,1,0:T(8,128)} %param.15) | copy-start | bytes 786436
  600.5 230.6 %all-to-all-start.1 = ((bf16[16,384,768]{2,1,0:T(8,128)(2,1)}), bf16[16,384,768]{2,1,0:T(8,128)(2,1)}, u32[]{:S(2)}, u32[]{:S(2)}) async-start(bf16[16,384,768]{2,1,0:T(8,128)(2,1)} %bitcast.62), calls=%async_computation.1 | async-start | bytes 18874368 | tf_op jit(solution)/shard_map/all_to_all | solution.py:101
  605.4 158.6 %all-gather.2.cloned.1.call-start = ((), (), s32[]{:S(2)}) async-start(), calls=%async_computation.2 | async-start | bytes 3342336 | tf_op jit(solution)/shard_map/all_gather | solution.py:108
  764.0 92.2 %collective-permute-start = (bf16[6144,256]{1,0:T(8,128)(2,1)}, bf16[6144,256]{1,0:T(8,128)(2,1)}, u32[]{:S(2)}, u32[]{:S(2)}) collective-permute-start(bf16[6144,256]{1,0:T(8,128)(2,1)} %all-gather.2.cloned.1.call-done), channel_id=1, source_target_pairs={{0,16},{16,0},{1,17},{17,1},{2,18},{18,2},{3,19},{19,3},{4,20},{20... | collective-permute-start | bytes 9437192 | tf_op jit(solution)/shard_map/ppermute | solution.py:10
  843.3 12.9 %copy-start.3 = (bf16[6144,256]{1,0:T(8,128)(2,1)S(1)}, bf16[6144,256]{1,0:T(8,128)(2,1)}, u32[]{:S(2)}) copy-start(bf16[6144,256]{1,0:T(8,128)(2,1)} %all-gather.2.cloned.1.call-done) | copy-start | bytes 9437188
  856.2 20.5 %copy-start.1 = (f32[1,256,256]{2,1,0:T(8,128)S(1)}, f32[1,256,256]{2,1,0:T(8,128)}, u32[]{:S(2)}) copy-start(f32[1,256,256]{2,1,0:T(8,128)} %param.10) | copy-start | bytes 786436
Sparse Core Ops, SparseCore 0:
  608.6 155.3 all-gather.1
